TPU v7x, 128 devices: a whole 4x4x4 slice. The times are simulated.
128 devices in a mesh: group: 8 (over x, z_hi), space: 16 (over y, z_lo, core).
Axes of the slice: x: 4, y: 4, z: 4 (z_hi: 2, z_lo: 2; z = z_hi * 2 + z_lo), core: 2. Of those that a mesh axis runs over, the one named last changes fastest.
Arguments:
- prev_field: float32 [8, 256, 256, 256], P('group', 'space'), may hold values from -6 to 6
- curr_field: float32 [8, 256, 256, 256], P('group', 'space'), may hold values from -6 to 6
- coefficient: float32 [256, 256, 256], P('space'), may hold values from 0.05 to 0.2
- recordings: float32 [8, 2, 512], P('group'), may hold values from -24 to 24
- receivers: int32 [8, 512], P('group'), may hold values from 0 to 16777215
- image_in: float32 [128, 128, 128], P('space', 'group'), may hold values from -6 to 6
Outputs:
- final_field: float32 [8, 256, 256, 256], P('group', 'space')
- image_out: float32 [128, 128, 128], P('space', 'group')
All inputs are finite; a program needn't handle non-finite values.
Results may differ from a plain program's by a relative error of at most 0.00002.
Values sent between devices are 32-bit elements; how exact they have to be, the bound alone decides.
A program may use at most 128 MiB of HBM per device.

v0:
```python
import jax
import jax.numpy as jnp
from jax import lax
from jax.sharding import PartitionSpec as P

STEPS = 2
DEC = 2
COEF = (-205.0 / 72.0, 8.0 / 5.0, -1.0 / 5.0, 8.0 / 315.0, -1.0 / 560.0)


def with_halo(block, sides, width):
    for axis, dim in sides:
        count = lax.axis_size(axis)
        forward = [(i, i + 1) for i in range(count - 1)]
        backward = [(target, source) for source, target in forward]
        low = lax.ppermute(
            lax.slice_in_dim(block, block.shape[dim] - width, None, axis=dim), axis, forward
        )
        high = lax.ppermute(lax.slice_in_dim(block, 0, width, axis=dim), axis, backward)
        block = jnp.concatenate([low, block, high], axis=dim)
    return block


def laplace(zpadded):
    nz = zpadded.shape[0] - 8
    nx = zpadded.shape[1]
    ny = zpadded.shape[2]
    full = jnp.pad(zpadded, ((0, 0), (4, 4), (4, 4)))
    centre = zpadded[4 : 4 + nz]
    total = 3.0 * COEF[0] * centre
    for j in range(1, 5):
        side = zpadded[4 + j : 4 + j + nz] + zpadded[4 - j : 4 - j + nz]
        side = (
            side
            + full[4 : 4 + nz, 4 + j : 4 + j + nx, 4 : 4 + ny]
            + full[4 : 4 + nz, 4 - j : 4 - j + nx, 4 : 4 + ny]
        )
        side = (
            side
            + full[4 : 4 + nz, 4 : 4 + nx, 4 + j : 4 + j + ny]
            + full[4 : 4 + nz, 4 : 4 + nx, 4 - j : 4 - j + ny]
        )
        total = total + COEF[j] * side
    return total


def inject(nxt, coef_planes, first_plane, record_now, index):
    plane_size = nxt.shape[1] * nxt.shape[2]
    planes = nxt.shape[0]
    zpos = index // plane_size - first_plane
    valid = (zpos >= 0) & (zpos < planes)
    local = jnp.where(valid, zpos * plane_size + index % plane_size, 0)
    amount = jnp.where(valid, coef_planes.reshape(-1)[local] * record_now, 0.0)
    return nxt.reshape(-1).at[local].add(amount).reshape(nxt.shape)


def geo_mean(fields):
    return jnp.exp(jnp.mean(jnp.log(1.0 + fields * fields), axis=0)) - 1.0


def on_device(prev_field, curr_field, coefficient, recordings, receivers, image_in):
    prev = prev_field[0]
    curr = curr_field[0]
    record = recordings[0]
    index = receivers[0]
    depth = curr.shape[0]
    slab = lax.axis_index("space")
    for step in range(STEPS):
        padded = with_halo(curr, (("space", 0),), 4)
        nxt = 2.0 * curr - prev + coefficient * laplace(padded)
        nxt = inject(nxt, coefficient, slab * depth, record[step], index)
        prev, curr = (curr, nxt)
    sample = curr[::DEC, ::DEC, ::DEC]
    update = geo_mean(
        lax.all_to_all(sample[None], "group", split_axis=2, concat_axis=0, tiled=True)
    )
    return (curr[None], image_in + update)


def solution(mesh):
    placed = (
        P("group", "space", None, None),
        P("group", "space", None, None),
        P("space", None, None),
        P("group", None, None),
        P("group", None),
        P("space", "group", None),
    )
    return jax.shard_map(
        on_device,
        mesh=mesh,
        in_specs=placed,
        out_specs=(P("group", "space", None, None), P("space", "group", None)),
        check_vma=False,
    )
```

profile of v0, /device:TPU:48, one launch (start us, length us, event | category | flops | bytes accessed | tf_op | source)
XLA Modules:
  0.0 247.5 jit_solution(16478315855580566975)
XLA Ops:
  0.6 2.7 %slice_bitcast_fusion.1 = (f32[4,256,256]{2,1,0:T(8,128)}, f32[4,256,256]{2,1,0:T(8,128)S(1)}) fusion(f32[1,16,256,256]{3,2,1,0:T(8,128)} %param.7), kind=kLoop, calls=%fused_computation.96 | loop fusion | bytes 4194304 | tf_op jit(solution)/shard_map/slice | solution.py:19
  3.3 1.9 collective-permute-start
  5.3 2.4 collective-permute-start.1
  7.7 0.0 copy-start.4
  7.7 0.0 copy-start.5
  7.7 6.4 %copy.13 = f32[512,2,8,128]{3,1,2,0:T(2,128)} copy(f32[512,2,8,128]{3,2,1,0:T(8,128)} %bitcast.41) | data formatting | bytes 8388608
  14.1 0.0 copy-done.4
  14.1 20.1 %gather_fusion = f32[512]{0:T(512)S(1)} fusion(f32[1048576]{0:T(1024)} %bitcast.44, s32[1024]{0:T(1024)S(1)} %pad_clamp_fusion), kind=kCustom, calls=%fused_computation | custom fusion | bytes 6144 | tf_op jit(solution)/shard_map/gather | solution.py:53
  34.2 0.0 copy-done.5
  34.2 0.0 collective-permute-done
  34.2 0.0 collective-permute-done.1
  34.2 8.7 %select_maximum_fusion.2 = f32[24,264,264]{2,1,0:T(8,128)} fusion(f32[4,256,256]{2,1,0:T(8,128)S(1)} %collective-permute-done, f32[16,256,256]{2,1,0:T(8,128)} %bitcast.38, f32[4,256,256]{2,1,0:T(8,128)S(1)} %collective-permute-done.1), kind=kLoop, calls=%fused_computation.9 | loop fusion | flops 25090560 | bytes 12982272 | tf_op jit(solution)/shard_map/concatenate | solution.py:20
  43.0 71.2 %fusion.13 = f32[16,256,256]{2,1,0:T(8,128)} fusion(f32[16,256,256]{2,1,0:T(8,128)} %param.8, f32[16,256,256]{2,1,0:T(8,128)} %bitcast.39, f32[4,256,256]{2,1,0:T(8,128)S(1)} %collective-permute-done.1, f32[4,256,256]{2,1,0:T(8,128)S(1)} %collective-permute-done, f32[24,264,264]{2,1,0:T(8,128)} %select_maximum_fusion.2, f32[1,16,256,256]{3,2,1,0:T(8,128)} %param.6), kind=kLoop, calls=%fused_computation.36 | loop fusion | flops 42991616 | bytes 85983232 | tf_op jit(solution)/shard_map/add | solution.py:70
  114.1 6.3 %copy.12 = f32[512,2,8,128]{3,1,2,0:T(2,128)} copy(f32[512,2,8,128]{3,2,1,0:T(8,128)} %bitcast.43) | data formatting | bytes 8388608
  120.4 8.0 %scatter_fusion = f32[1048576]{0:T(1024)} fusion(f32[1048576]{0:T(1024)} %bitcast.40, s32[512]{0:T(512)S(1)} %bitcast.48, f32[512]{0:T(512)S(1)} %get-tuple-element.11), kind=kCustom, calls=%fused_computation.1 | custom fusion | flops 512 | bytes 8192 | tf_op jit(solution)/shard_map/scatter-add | solution.py:54
  128.4 1.7 fusion.49
  130.1 1.3 slice.244
  131.4 3.5 %collective-permute-start.3 = (f32[4,256,256]{2,1,0:T(8,128)}, f32[4,256,256]{2,1,0:T(8,128)S(1)}, u32[]{:S(2)}, u32[]{:S(2)}) collective-permute-start(f32[4,256,256]{2,1,0:T(8,128)} %slice.244), channel_id=1, source_target_pairs={{0,1},{1,2},{2,3},{3,4},{4,5},{5,6},{6,7},{7,8},{8,9},{9,10},{10,1... | collective-permute-start | bytes 3145736 | tf_op jit(solution)/shard_map/ppermute | solution.py:16
  134.8 0.3 slice.241
  135.1 2.1 collective-permute-start.2
  137.2 5.2 %reshape.178 = f32[16,256,256]{2,1,0:T(8,128)} reshape(f32[1048576]{0:T(1024)} %scatter_fusion) | data formatting | bytes 8388608 | tf_op jit(solution)/shard_map/reshape | solution.py:54
  142.4 16.5 %collective-permute-done.3 = f32[4,256,256]{2,1,0:T(8,128)S(1)} collective-permute-done((f32[4,256,256]{2,1,0:T(8,128)}, f32[4,256,256]{2,1,0:T(8,128)S(1)}, u32[]{:S(2)}, u32[]{:S(2)}) %collective-permute-start.3) | collective-permute-done | bytes 1048608 | tf_op jit(solution)/shard_map/ppermute | solution.py:16
  158.9 0.0 copy-start.2
  158.9 0.1 constant_dynamic-update-slice_fusion.3
  159.0 0.0 copy-start
  159.0 3.6 %constant_dynamic-update-slice_fusion.1 = (f32[20,256,256]{2,1,0:T(8,128)S(1)}, f32[20,256,256]{2,1,0:T(8,128)S(1)}) fusion(f32[16,256,256]{2,1,0:T(8,128)} %reshape.178, f32[20,256,256]{2,1,0:T(8,128)S(1)} %constant_dynamic-update-slice_fusion.3), kind=kLoop, calls=%fused_computation.101 | loop fusion | bytes 12582912
  162.6 0.0 copy-done.2
  162.7 0.0 copy-start.1
  162.7 0.0 collective-permute-done.2
  162.7 0.1 copy-done
  162.8 6.4 %select_maximum_fusion = f32[24,264,264]{2,1,0:T(8,128)S(1)} fusion(f32[4,256,256]{2,1,0:T(8,128)} %collective-permute-done.2, f32[16,256,256]{2,1,0:T(8,128)S(1)} %copy-done, f32[4,256,256]{2,1,0:T(8,128)} %copy-done.2), kind=kLoop, calls=%fused_computation.7 | loop fusion | flops 25090560 | bytes 12982272 | tf_op jit(solution)/shard_map/concatenate | solution.py:20
  169.2 1.3 constant_dynamic-update-slice_fusion
  170.5 0.0 copy-done.1
  170.5 20.0 %fusion.36 = f32[16,256,256]{2,1,0:T(8,128)} fusion(f32[16,256,256]{2,1,0:T(8,128)} %param.8, f32[24,264,264]{2,1,0:T(8,128)S(1)} %select_maximum_fusion, f32[20,256,256]{2,1,0:T(8,128)} %copy-done.1, f32[20,256,256]{2,1,0:T(8,128)S(1)} %constant_dynamic-update-slice_fusion, f32[16,256,256]{2,1,0:T(8,128)S(1)} %copy-done, f32[1,16,256,256]{3,2,1,0:T(8,128)} %param.7), kind=kLoop, calls=%fused_computation.60 | loop fusion | flops 34603008 | bytes 117440512 | tf_op jit(solution)/shard_map/add | solution.py:70
  190.6 6.3 %copy.14 = f32[512,2,8,128]{3,1,2,0:T(2,128)} copy(f32[512,2,8,128]{3,2,1,0:T(8,128)} %bitcast.42) | data formatting | bytes 8388608
  196.8 8.0 %scatter_fusion.1 = f32[1048576]{0:T(1024)} fusion(f32[1048576]{0:T(1024)} %bitcast.37, s32[512]{0:T(512)S(1)} %bitcast.49, f32[512]{0:T(512)S(1)} %get-tuple-element.10), kind=kCustom, calls=%fused_computation.2 | custom fusion | flops 512 | bytes 8192 | tf_op jit(solution)/shard_map/scatter-add | solution.py:54
  204.8 5.2 %reshape.180 = f32[16,256,256]{2,1,0:T(8,128)} reshape(f32[1048576]{0:T(1024)} %scatter_fusion.1) | data formatting | bytes 8388608 | tf_op jit(solution)/shard_map/reshape | solution.py:54
  210.0 18.9 %slice.269 = f32[8,128,128]{2,1,0:T(8,128)S(1)} slice(f32[16,256,256]{2,1,0:T(8,128)} %reshape.180), slice={[0:16:2], [0:256:2], [0:256:2]} | slice | bytes 1048576 | tf_op jit(solution)/shard_map/slice | solution.py:73
  228.9 1.1 copy.9
  230.0 7.0 %all-to-all-start = ((f32[1,8,128,128]{3,1,0,2:T(8,128)}), f32[1,8,128,128]{3,1,0,2:T(8,128)S(1)}, u32[]{:S(2)}, u32[]{:S(2)}) async-start(f32[1,8,128,128]{3,1,0,2:T(8,128)} %copy.9), calls=%async_computation | async-start | bytes 1048576 | tf_op jit(solution)/shard_map/all_to_all | solution.py:75
  237.0 0.0 copy-start.3
  237.0 5.2 %broadcast_in_dim_reshape.3 = f32[1,16,256,256]{3,2,1,0:T(8,128)} reshape(f32[1048576]{0:T(1024)} %scatter_fusion.1) | data formatting | bytes 8388608 | tf_op jit(solution)/shard_map/broadcast_in_dim;reshape | solution.py:77
  242.3 4.5 %all-to-all-done = f32[1,8,128,128]{3,1,0,2:T(8,128)S(1)} async-done(((f32[1,8,128,128]{3,1,0,2:T(8,128)}), f32[1,8,128,128]{3,1,0,2:T(8,128)S(1)}, u32[]{:S(2)}, u32[]{:S(2)}) %all-to-all-start) | async-done | bytes 524320 | tf_op jit(solution)/shard_map/all_to_all | solution.py:75
  246.7 0.1 add_log_fusion
  246.8 0.0 copy-done.3
  246.9 0.6 copy.11
  (6 shorter events, 0.1 us)
Async XLA Ops:
  3.3 30.9 %collective-permute-start = (f32[4,256,256]{2,1,0:T(8,128)}, f32[4,256,256]{2,1,0:T(8,128)S(1)}, u32[]{:S(2)}, u32[]{:S(2)}) collective-permute-start(f32[4,256,256]{2,1,0:T(8,128)} %get-tuple-element.8), channel_id=1, source_target_pairs={{1,0},{2,1},{3,2},{4,3},{5,4},{6,5},{7,6},{8,7},{9,8},{10,9},{11,1... | collective-permute-start | bytes 3145736 | tf_op jit(solution)/shard_map/ppermute | solution.py:19
  5.3 29.0 %collective-permute-start.1 = (f32[4,256,256]{2,1,0:T(8,128)S(1)}, f32[4,256,256]{2,1,0:T(8,128)S(1)}, u32[]{:S(2)}, u32[]{:S(2)}) collective-permute-start(f32[4,256,256]{2,1,0:T(8,128)S(1)} %get-tuple-element.9), channel_id=1, source_target_pairs={{0,1},{1,2},{2,3},{3,4},{4,5},{5,6},{6,7},{7,8},{8,9},{9,10},{10,1... | collective-permute-start | bytes 3145736 | tf_op jit(solution)/shard_map/ppermute | solution.py:16
  7.7 6.4 %copy-start.4 = (s32[1,512]{1,0:T(1,128)S(1)}, s32[1,512]{1,0:T(1,128)}, u32[]{:S(2)}) copy-start(s32[1,512]{1,0:T(1,128)} %param.10) | copy-start | bytes 6148
  7.7 26.5 %copy-start.5 = (f32[1,2,512]{2,1,0:T(2,128)S(1)}, f32[1,2,512]{2,1,0:T(2,128)}, u32[]{:S(2)}) copy-start(f32[1,2,512]{2,1,0:T(2,128)} %param.9) | copy-start | bytes 12292
  131.4 27.6 %collective-permute-start.3 = (f32[4,256,256]{2,1,0:T(8,128)}, f32[4,256,256]{2,1,0:T(8,128)S(1)}, u32[]{:S(2)}, u32[]{:S(2)}) collective-permute-start(f32[4,256,256]{2,1,0:T(8,128)} %slice.244), channel_id=1, source_target_pairs={{0,1},{1,2},{2,3},{3,4},{4,5},{5,6},{6,7},{7,8},{8,9},{9,10},{10,1... | collective-permute-start | bytes 3145736 | tf_op jit(solution)/shard_map/ppermute | solution.py:16
  135.1 27.5 %collective-permute-start.2 = (f32[4,256,256]{2,1,0:T(8,128)S(1)}, f32[4,256,256]{2,1,0:T(8,128)}, u32[]{:S(2)}, u32[]{:S(2)}) collective-permute-start(f32[4,256,256]{2,1,0:T(8,128)S(1)} %slice.241), channel_id=1, source_target_pairs={{1,0},{2,1},{3,2},{4,3},{5,4},{6,5},{7,6},{8,7},{9,8},{10,9},{11,1... | collective-permute-start | bytes 3145736 | tf_op jit(solution)/shard_map/ppermute | solution.py:19
  158.9 3.7 %copy-start.2 = (f32[4,256,256]{2,1,0:T(8,128)}, f32[4,256,256]{2,1,0:T(8,128)S(1)}, u32[]{:S(2)}) copy-start(f32[4,256,256]{2,1,0:T(8,128)S(1)} %collective-permute-done.3) | copy-start | bytes 3145732
  159.0 3.8 %copy-start = (f32[16,256,256]{2,1,0:T(8,128)S(1)}, f32[16,256,256]{2,1,0:T(8,128)}, u32[]{:S(2)}) copy-start(f32[16,256,256]{2,1,0:T(8,128)} %reshape.178) | copy-start | bytes 12582916
  162.7 7.9 %copy-start.1 = (f32[20,256,256]{2,1,0:T(8,128)}, f32[20,256,256]{2,1,0:T(8,128)S(1)}, u32[]{:S(2)}) copy-start(f32[20,256,256]{2,1,0:T(8,128)S(1)} %get-tuple-element.5) | copy-start | bytes 15728644
  230.0 16.7 %all-to-all-start = ((f32[1,8,128,128]{3,1,0,2:T(8,128)}), f32[1,8,128,128]{3,1,0,2:T(8,128)S(1)}, u32[]{:S(2)}, u32[]{:S(2)}) async-start(f32[1,8,128,128]{3,1,0,2:T(8,128)} %copy.9), calls=%async_computation | async-start | bytes 1048576 | tf_op jit(solution)/shard_map/all_to_all | solution.py:75
  237.0 9.8 %copy-start.3 = (f32[8,16,128]{2,1,0:T(8,128)S(1)}, f32[8,16,128]{2,1,0:T(8,128)}, u32[]{:S(2)}) copy-start(f32[8,16,128]{2,1,0:T(8,128)} %param.11) | copy-start | bytes 196612
where the time goes:
time: 249 us; the launch traced here: 248 us
  other arithmetic  123 us (49%)
  local copies, waits for them, and re-layouts  86.2 us (35%)
  waiting for transfers between devices  21 us (8%)
  starting transfers between devices  16.9 us (7%)
    add x2, other arithmetic, on_device(): nxt = 2.0 * curr - prev + coefficient * laplace(padded)  91.2 us
    unnamed x18, local copies, waits for them, and re-layouts  23.4 us
    gather x1, local copies, waits for them, and re-layouts, inject(): amount = jnp.where(valid, coef_planes.reshape(-1)[local] * record_now, 0.0)  20.1 us
    slice x1, local copies, waits for them, and re-layouts, on_device(): sample = curr[::DEC, ::DEC, ::DEC]  18.9 us
    ppermute x2, waiting for transfers between devices, with_halo(): lax.ppermute(lax.slice_in_dim(block, block.shape[dim] - width, None, axis...  16.5 us
    scatter-add x2, other arithmetic, inject(): return nxt.reshape(-1).at[local].add(amount).reshape(nxt.shape)  16 us
    concatenate x2, other arithmetic, with_halo(): block = jnp.concatenate([low, block, high], axis=dim)  15.2 us
    reshape x2, local copies, waits for them, and re-layouts, inject(): return nxt.reshape(-1).at[local].add(amount).reshape(nxt.shape)  10.4 us
  transfers between devices with their start and end apart: 5, of which 2 were waited for; matrix products, arithmetic and copies ran while one was open for 17% of the time, Pallas kernels for 0%

commit v1 on v0

--- a/solution.py
+++ b/solution.py
@@ -72,7 +72,12 @@
         prev, curr = (curr, nxt)
     sample = curr[::DEC, ::DEC, ::DEC]
     update = geo_mean(
-        lax.all_to_all(sample[None], "group", split_axis=2, concat_axis=0, tiled=True)
+        jnp.concatenate(
+            lax.all_to_all(
+                jnp.stack(jnp.split(sample[None], lax.axis_size("group"), axis=2)), "group", 0, 0
+            ),
+            axis=0,
+        )
     )
     return (curr[None], image_in + update)
 

time: 249 us -> 253 us (1.016)
  local copies, waits for them, and re-layouts: 86.2 us -> 89.5 us
    unnamed x18 -> x24, local copies, waits for them, and re-layouts: 23.4 us -> 27.1 us
  transfers between devices with their start and end apart: 5 -> 5, of which waited for: 2 -> 2; matrix products, arithmetic and copies ran while one was open for 17% -> 16% of each run, Pallas kernels for 0% -> 0%
where the time goes in v1:
time: 253 us; the launch traced here: 251 us
  other arithmetic  123 us (49%)
  local copies, waits for them, and re-layouts  89.5 us (35%)
  waiting for transfers between devices  21 us (8%)
  starting transfers between devices  16.9 us (7%)
    add x2, other arithmetic, on_device(): nxt = 2.0 * curr - prev + coefficient * laplace(padded)  91.2 us
    unnamed x24, local copies, waits for them, and re-layouts  27.1 us
    gather x1, local copies, waits for them, and re-layouts, inject(): amount = jnp.where(valid, coef_planes.reshape(-1)[local] * record_now, 0.0)  20.1 us
    slice x1, local copies, waits for them, and re-layouts, on_device(): sample = curr[::DEC, ::DEC, ::DEC]  18.9 us
    ppermute x2, waiting for transfers between devices, with_halo(): lax.ppermute(lax.slice_in_dim(block, block.shape[dim] - width, None, axis...  16.5 us
    scatter-add x2, other arithmetic, inject(): return nxt.reshape(-1).at[local].add(amount).reshape(nxt.shape)  16 us
    concatenate x2, other arithmetic, with_halo(): block = jnp.concatenate([low, block, high], axis=dim)  15.2 us
    reshape x2, local copies, waits for them, and re-layouts, inject(): return nxt.reshape(-1).at[local].add(amount).reshape(nxt.shape)  10.4 us
  transfers between devices with their start and end apart: 5, of which 2 were waited for; matrix products, arithmetic and copies ran while one was open for 16% of the time, Pallas kernels for 0%

profile of v1, /device:TPU:48, one launch (start us, length us, event | category | flops | bytes accessed | tf_op | source)
XLA Modules:
  0.0 251.4 jit_solution(16184973800624710082)
XLA Ops:
  0.6 2.7 %slice_bitcast_fusion.1 = (f32[4,256,256]{2,1,0:T(8,128)}, f32[4,256,256]{2,1,0:T(8,128)S(1)}) fusion(f32[1,16,256,256]{3,2,1,0:T(8,128)} %param.7), kind=kLoop, calls=%fused_computation.96 | loop fusion | bytes 4194304 | tf_op jit(solution)/shard_map/slice | solution.py:19
  3.3 1.9 collective-permute-start
  5.3 2.4 collective-permute-start.1
  7.7 0.0 copy-start.4
  7.7 0.0 copy-start.5
  7.7 6.4 %copy.9 = f32[512,2,8,128]{3,1,2,0:T(2,128)} copy(f32[512,2,8,128]{3,2,1,0:T(8,128)} %bitcast.72) | data formatting | bytes 8388608
  14.1 0.0 copy-done.4
  14.1 20.1 %gather_fusion = f32[512]{0:T(512)S(1)} fusion(f32[1048576]{0:T(1024)} %bitcast.75, s32[1024]{0:T(1024)S(1)} %pad_clamp_fusion), kind=kCustom, calls=%fused_computation | custom fusion | bytes 6144 | tf_op jit(solution)/shard_map/gather | solution.py:53
  34.2 0.0 copy-done.5
  34.2 0.0 collective-permute-done
  34.2 0.0 collective-permute-done.1
  34.2 8.7 %select_maximum_fusion.2 = f32[24,264,264]{2,1,0:T(8,128)} fusion(f32[4,256,256]{2,1,0:T(8,128)S(1)} %collective-permute-done, f32[16,256,256]{2,1,0:T(8,128)} %bitcast.69, f32[4,256,256]{2,1,0:T(8,128)S(1)} %collective-permute-done.1), kind=kLoop, calls=%fused_computation.9 | loop fusion | flops 25090560 | bytes 12982272 | tf_op jit(solution)/shard_map/concatenate | solution.py:20
  43.0 71.2 %fusion.13 = f32[16,256,256]{2,1,0:T(8,128)} fusion(f32[16,256,256]{2,1,0:T(8,128)} %param.8, f32[16,256,256]{2,1,0:T(8,128)} %bitcast.70, f32[4,256,256]{2,1,0:T(8,128)S(1)} %collective-permute-done.1, f32[4,256,256]{2,1,0:T(8,128)S(1)} %collective-permute-done, f32[24,264,264]{2,1,0:T(8,128)} %select_maximum_fusion.2, f32[1,16,256,256]{3,2,1,0:T(8,128)} %param.6), kind=kLoop, calls=%fused_computation.36 | loop fusion | flops 42991616 | bytes 85983232 | tf_op jit(solution)/shard_map/add | solution.py:70
  114.1 6.3 %copy.8 = f32[512,2,8,128]{3,1,2,0:T(2,128)} copy(f32[512,2,8,128]{3,2,1,0:T(8,128)} %bitcast.74) | data formatting | bytes 8388608
  120.4 8.0 %scatter_fusion = f32[1048576]{0:T(1024)} fusion(f32[1048576]{0:T(1024)} %bitcast.71, s32[512]{0:T(512)S(1)} %bitcast.85, f32[512]{0:T(512)S(1)} %get-tuple-element.9), kind=kCustom, calls=%fused_computation.1 | custom fusion | flops 512 | bytes 8192 | tf_op jit(solution)/shard_map/scatter-add | solution.py:54
  128.4 1.7 fusion.57
  130.1 1.3 slice.244
  131.4 3.5 %collective-permute-start.3 = (f32[4,256,256]{2,1,0:T(8,128)}, f32[4,256,256]{2,1,0:T(8,128)S(1)}, u32[]{:S(2)}, u32[]{:S(2)}) collective-permute-start(f32[4,256,256]{2,1,0:T(8,128)} %slice.244), channel_id=1, source_target_pairs={{0,1},{1,2},{2,3},{3,4},{4,5},{5,6},{6,7},{7,8},{8,9},{9,10},{10,1... | collective-permute-start | bytes 3145736 | tf_op jit(solution)/shard_map/ppermute | solution.py:16
  134.8 0.3 slice.241
  135.1 2.1 collective-permute-start.2
  137.2 5.2 %reshape.176 = f32[16,256,256]{2,1,0:T(8,128)} reshape(f32[1048576]{0:T(1024)} %scatter_fusion) | data formatting | bytes 8388608 | tf_op jit(solution)/shard_map/reshape | solution.py:54
  142.4 16.5 %collective-permute-done.3 = f32[4,256,256]{2,1,0:T(8,128)S(1)} collective-permute-done((f32[4,256,256]{2,1,0:T(8,128)}, f32[4,256,256]{2,1,0:T(8,128)S(1)}, u32[]{:S(2)}, u32[]{:S(2)}) %collective-permute-start.3) | collective-permute-done | bytes 1048608 | tf_op jit(solution)/shard_map/ppermute | solution.py:16
  158.9 0.0 copy-start.2
  158.9 0.1 constant_dynamic-update-slice_fusion.3
  159.0 0.0 copy-start
  159.0 3.6 %constant_dynamic-update-slice_fusion.1 = (f32[20,256,256]{2,1,0:T(8,128)S(1)}, f32[20,256,256]{2,1,0:T(8,128)S(1)}) fusion(f32[16,256,256]{2,1,0:T(8,128)} %reshape.176, f32[20,256,256]{2,1,0:T(8,128)S(1)} %constant_dynamic-update-slice_fusion.3), kind=kLoop, calls=%fused_computation.116 | loop fusion | bytes 12582912
  162.6 0.0 copy-done.2
  162.7 0.0 copy-start.1
  162.7 0.0 collective-permute-done.2
  162.7 0.1 copy-done
  162.8 6.4 %select_maximum_fusion = f32[24,264,264]{2,1,0:T(8,128)S(1)} fusion(f32[4,256,256]{2,1,0:T(8,128)} %collective-permute-done.2, f32[16,256,256]{2,1,0:T(8,128)S(1)} %copy-done, f32[4,256,256]{2,1,0:T(8,128)} %copy-done.2), kind=kLoop, calls=%fused_computation.7 | loop fusion | flops 25090560 | bytes 12982272 | tf_op jit(solution)/shard_map/concatenate | solution.py:20
  169.2 1.3 constant_dynamic-update-slice_fusion
  170.5 0.0 copy-done.1
  170.5 20.0 %fusion.36 = f32[16,256,256]{2,1,0:T(8,128)} fusion(f32[16,256,256]{2,1,0:T(8,128)} %param.8, f32[24,264,264]{2,1,0:T(8,128)S(1)} %select_maximum_fusion, f32[20,256,256]{2,1,0:T(8,128)} %copy-done.1, f32[20,256,256]{2,1,0:T(8,128)S(1)} %constant_dynamic-update-slice_fusion, f32[16,256,256]{2,1,0:T(8,128)S(1)} %copy-done, f32[1,16,256,256]{3,2,1,0:T(8,128)} %param.7), kind=kLoop, calls=%fused_computation.60 | loop fusion | flops 34603008 | bytes 117440512 | tf_op jit(solution)/shard_map/add | solution.py:70
  190.6 6.3 %copy.10 = f32[512,2,8,128]{3,1,2,0:T(2,128)} copy(f32[512,2,8,128]{3,2,1,0:T(8,128)} %bitcast.73) | data formatting | bytes 8388608
  196.8 8.0 %scatter_fusion.1 = f32[1048576]{0:T(1024)} fusion(f32[1048576]{0:T(1024)} %bitcast.68, s32[512]{0:T(512)S(1)} %bitcast.86, f32[512]{0:T(512)S(1)} %get-tuple-element.8), kind=kCustom, calls=%fused_computation.2 | custom fusion | flops 512 | bytes 8192 | tf_op jit(solution)/shard_map/scatter-add | solution.py:54
  204.8 5.2 %reshape.178 = f32[16,256,256]{2,1,0:T(8,128)} reshape(f32[1048576]{0:T(1024)} %scatter_fusion.1) | data formatting | bytes 8388608 | tf_op jit(solution)/shard_map/reshape | solution.py:54
  210.0 18.9 %slice.269 = f32[8,128,128]{2,1,0:T(8,128)S(1)} slice(f32[16,256,256]{2,1,0:T(8,128)} %reshape.178), slice={[0:16:2], [0:256:2], [0:256:2]} | slice | bytes 1048576 | tf_op jit(solution)/shard_map/slice | solution.py:73
  228.9 0.6 fusion.52
  229.5 0.6 fusion.51
  230.1 0.6 fusion.50
  230.7 0.6 fusion.49
  231.4 0.6 fusion.48
  232.0 0.6 fusion.47
  232.6 0.6 fusion.46
  233.3 0.6 fusion.45
  233.9 7.0 %all-to-all-start = ((f32[8,1,8,16,128]{4,3,2,1,0:T(8,128)}), f32[8,1,8,16,128]{4,3,2,1,0:T(8,128)S(1)}, u32[]{:S(2)}, u32[]{:S(2)}) async-start(f32[8,1,8,16,128]{4,3,2,1,0:T(8,128)} %fusion.45), calls=%async_computation | async-start | bytes 1048576 | tf_op jit(solution)/shard_map/all_to_all | solution.py:76
  241.0 0.0 copy-start.3
  241.0 5.2 %broadcast_in_dim_reshape.3 = f32[1,16,256,256]{3,2,1,0:T(8,128)} reshape(f32[1048576]{0:T(1024)} %scatter_fusion.1) | data formatting | bytes 8388608 | tf_op jit(solution)/shard_map/broadcast_in_dim;reshape | solution.py:82
  246.2 4.5 %all-to-all-done = f32[8,1,8,16,128]{4,3,2,1,0:T(8,128)S(1)} async-done(((f32[8,1,8,16,128]{4,3,2,1,0:T(8,128)}), f32[8,1,8,16,128]{4,3,2,1,0:T(8,128)S(1)}, u32[]{:S(2)}, u32[]{:S(2)}) %all-to-all-start) | async-done | bytes 524320 | tf_op jit(solution)/shard_map/all_to_all | solution.py:76
  250.6 0.1 log_reduce_fusion
  250.7 0.0 copy-done.3
  250.8 0.6 add_add_fusion
  (4 shorter events, 0.1 us)
Async XLA Ops:
  3.3 30.9 %collective-permute-start = (f32[4,256,256]{2,1,0:T(8,128)}, f32[4,256,256]{2,1,0:T(8,128)S(1)}, u32[]{:S(2)}, u32[]{:S(2)}) collective-permute-start(f32[4,256,256]{2,1,0:T(8,128)} %get-tuple-element.6), channel_id=1, source_target_pairs={{1,0},{2,1},{3,2},{4,3},{5,4},{6,5},{7,6},{8,7},{9,8},{10,9},{11,1... | collective-permute-start | bytes 3145736 | tf_op jit(solution)/shard_map/ppermute | solution.py:19
  5.3 29.0 %collective-permute-start.1 = (f32[4,256,256]{2,1,0:T(8,128)S(1)}, f32[4,256,256]{2,1,0:T(8,128)S(1)}, u32[]{:S(2)}, u32[]{:S(2)}) collective-permute-start(f32[4,256,256]{2,1,0:T(8,128)S(1)} %get-tuple-element.7), channel_id=1, source_target_pairs={{0,1},{1,2},{2,3},{3,4},{4,5},{5,6},{6,7},{7,8},{8,9},{9,10},{10,1... | collective-permute-start | bytes 3145736 | tf_op jit(solution)/shard_map/ppermute | solution.py:16
  7.7 6.4 %copy-start.4 = (s32[1,512]{1,0:T(1,128)S(1)}, s32[1,512]{1,0:T(1,128)}, u32[]{:S(2)}) copy-start(s32[1,512]{1,0:T(1,128)} %param.10) | copy-start | bytes 6148
  7.7 26.5 %copy-start.5 = (f32[1,2,512]{2,1,0:T(2,128)S(1)}, f32[1,2,512]{2,1,0:T(2,128)}, u32[]{:S(2)}) copy-start(f32[1,2,512]{2,1,0:T(2,128)} %param.9) | copy-start | bytes 12292
  131.4 27.6 %collective-permute-start.3 = (f32[4,256,256]{2,1,0:T(8,128)}, f32[4,256,256]{2,1,0:T(8,128)S(1)}, u32[]{:S(2)}, u32[]{:S(2)}) collective-permute-start(f32[4,256,256]{2,1,0:T(8,128)} %slice.244), channel_id=1, source_target_pairs={{0,1},{1,2},{2,3},{3,4},{4,5},{5,6},{6,7},{7,8},{8,9},{9,10},{10,1... | collective-permute-start | bytes 3145736 | tf_op jit(solution)/shard_map/ppermute | solution.py:16
  135.1 27.5 %collective-permute-start.2 = (f32[4,256,256]{2,1,0:T(8,128)S(1)}, f32[4,256,256]{2,1,0:T(8,128)}, u32[]{:S(2)}, u32[]{:S(2)}) collective-permute-start(f32[4,256,256]{2,1,0:T(8,128)S(1)} %slice.241), channel_id=1, source_target_pairs={{1,0},{2,1},{3,2},{4,3},{5,4},{6,5},{7,6},{8,7},{9,8},{10,9},{11,1... | collective-permute-start | bytes 3145736 | tf_op jit(solution)/shard_map/ppermute | solution.py:19
  158.9 3.7 %copy-start.2 = (f32[4,256,256]{2,1,0:T(8,128)}, f32[4,256,256]{2,1,0:T(8,128)S(1)}, u32[]{:S(2)}) copy-start(f32[4,256,256]{2,1,0:T(8,128)S(1)} %collective-permute-done.3) | copy-start | bytes 3145732
  159.0 3.8 %copy-start = (f32[16,256,256]{2,1,0:T(8,128)S(1)}, f32[16,256,256]{2,1,0:T(8,128)}, u32[]{:S(2)}) copy-start(f32[16,256,256]{2,1,0:T(8,128)} %reshape.176) | copy-start | bytes 12582916
  162.7 7.9 %copy-start.1 = (f32[20,256,256]{2,1,0:T(8,128)}, f32[20,256,256]{2,1,0:T(8,128)S(1)}, u32[]{:S(2)}) copy-start(f32[20,256,256]{2,1,0:T(8,128)S(1)} %get-tuple-element.3) | copy-start | bytes 15728644
  233.9 16.7 %all-to-all-start = ((f32[8,1,8,16,128]{4,3,2,1,0:T(8,128)}), f32[8,1,8,16,128]{4,3,2,1,0:T(8,128)S(1)}, u32[]{:S(2)}, u32[]{:S(2)}) async-start(f32[8,1,8,16,128]{4,3,2,1,0:T(8,128)} %fusion.45), calls=%async_computation | async-start | bytes 1048576 | tf_op jit(solution)/shard_map/all_to_all | solution.py:76
  241.0 9.8 %copy-start.3 = (f32[8,16,128]{2,1,0:T(8,128)S(1)}, f32[8,16,128]{2,1,0:T(8,128)}, u32[]{:S(2)}) copy-start(f32[8,16,128]{2,1,0:T(8,128)} %param.11) | copy-start | bytes 196612
